TPU v7x, 32 devices: a whole 2x2x4 slice. The times are simulated.
32 devices in a mesh: lat: 8 (over z, x), lon: 4 (over y, core).
Axes of the slice: x: 2, y: 2, z: 4, core: 2. Of those that a mesh axis runs over, the one named last changes fastest.
Arguments:
- adjoint_in: float32 [128, 128, 1024], P(None, 'lat', 'lon'), may hold values from -6 to 6
- obs_adjoint: float32 [65536, 128], P(('lat', 'lon')), may hold values from -6 to 6
- obs_owner: int32 [65536, 1], P(('lat', 'lon')), may hold values from 0 to 31; in each aligned block of 2048 rows (0 to 2047, 2048 to 4095, ...) at most 128 rows name the same one
- obs_column: int32 [65536], P(('lat', 'lon')), may hold values from 0 to 4095
- winds: float32 [3, 2, 32, 128, 1024], P(None, None, None, 'lat', 'lon'), may hold values from -0.3 to 0.3
- diffusion: float32 [128], replicated, may hold values from 0.03 to 0.12
Outputs:
- adjoint_out: float32 [128, 128, 1024], P(None, 'lat', 'lon')
Inputs may be any that keep to these rules, and one draw needn't show every extreme that they name: `obs_owner`: in each aligned block of 2048 observations (one shard's), no owner is named more than 128 times, a bound that some block reaches.
All inputs are finite; a program needn't handle non-finite values.
Results may differ from a plain program's by a relative error of at most 0.00002.
Values sent between devices are 32-bit elements; how exact they have to be, the bound alone decides.
A program may use at most 64 MiB of HBM per device.

v0:
```python
import functools

import jax
import jax.numpy as jnp
from jax import lax
from jax.experimental import pallas as pl
from jax.experimental.pallas import tpu as pltpu
from jax.sharding import PartitionSpec as P

STEPS = 3
LANES = 128
META = 8
JOIN = 4
TWIST = 13
UNROLL = 5
F32 = jnp.float32
BF16 = jnp.bfloat16
NT = (((1,), (1,)), ((), ()))


def halves(x):
    high = x.astype(BF16)
    return high, (x - high.astype(F32)).astype(BF16)


def kernel(
    n_lat, n_lon,
    obs_ref, owner_ref, column_ref, diffusion_ref, adj_ref, winds_ref, out_ref,
    obs, k_ref, half, wind_west, wind_south, pieces, rank_ref, send_v, recv_v, lhs,
    state_a, state_b, winds, row_halo, col_send, col_halo, wind_row, wind_send, wind_col,
    obs_sem, adj_sem, wind_sem, self_sem, sv_sem, rv_sem, hs_sem, hr_sem, ws_sem, wr_sem, out_sem,
):
    lat = lax.axis_index("lat")
    lon = lax.axis_index("lon")
    n = n_lat * n_lon
    me = lat * n_lon + lon
    rows, chan = obs.shape
    lat_rows, _, lon_cols = state_a.shape
    lev = winds.shape[3]
    fields = chan // lev
    lane = lax.broadcasted_iota(jnp.int32, (1, LANES), 1)

    def device(d):
        return (lax.div(d, n_lon), lax.rem(d, n_lon))

    def remote(src, dst, send, recv, to):
        return pltpu.make_async_remote_copy(
            src_ref=src, dst_ref=dst, send_sem=send, recv_sem=recv,
            device_id=to, device_id_type=pl.DeviceIdType.MESH,
        )

    width = 256
    blocks = rows // width

    def load_obs(b):
        span = pl.ds(b * width, width)
        return pltpu.make_async_copy(obs_ref.at[span], obs.at[span], obs_sem.at[b])

    for b in range(blocks):
        load_obs(b).start()

    barrier = pltpu.get_barrier_semaphore()

    def greet(k, _):
        pl.semaphore_signal(
            barrier, inc=1, device_id=device(lax.rem(me + k, n)),
            device_id_type=pl.DeviceIdType.MESH,
        )
        return 0

    lax.fori_loop(1, n, greet, 0)

    def load_row(l):
        return pltpu.make_async_copy(adj_ref.at[:, l, :], state_a.at[l], adj_sem.at[l])

    def load_wind(s, w, l):
        return pltpu.make_async_copy(
            winds_ref.at[s, w, :, l, :], winds.at[s, w, l], wind_sem.at[s, w, l]
        )

    def each_row(act):
        lax.fori_loop(0, lat_rows, lambda l, _: act(l) or 0, 0)

    def each_wind(act):
        for s in range(STEPS):
            for w in range(2):
                lax.fori_loop(0, lat_rows, lambda l, _: act(s, w, l) or 0, 0)

    each_wind(lambda s, w, l: load_wind(s, w, l).start())
    each_row(lambda l: load_row(l).start())

    below = lax.broadcasted_iota(jnp.int32, (width, width), 0)
    along = lax.broadcasted_iota(jnp.int32, (width, width), 1)
    before = jnp.where(below < along, 1.0, 0.0).astype(BF16)
    carry = jnp.zeros((n, 1), F32)
    owners = lax.broadcasted_iota(jnp.int32, (n, width), 0)
    sub = lax.broadcasted_iota(jnp.int32, (16, width), 0)
    for b in range(blocks):
        span = slice(b * width, (b + 1) * width)
        owner = owner_ref[:, span]
        hot = jnp.where(owners == owner, 1.0, 0.0)
        rank = jnp.dot(hot.astype(BF16), before, preferred_element_type=F32) + carry
        rank_ref[:, span] = jnp.sum(hot * rank, axis=0, keepdims=True).astype(jnp.int32) + owner * LANES
        carry = carry + jnp.sum(hot, axis=1, keepdims=True)
        column = column_ref[:, span]
        if lon_cols & (lon_cols - 1):
            row = jnp.floor((column.astype(F32) + 0.5) * (1.0 / lon_cols)).astype(jnp.int32)
        else:
            row = column >> (lon_cols.bit_length() - 1)
        turned = column - row * lon_cols + row + 1
        turned = jnp.where(turned >= lon_cols, turned - lon_cols, turned)
        pieces[2 * chan:, span] = jnp.where(
            sub == 0, row, jnp.where(sub == 1, turned, 0)
        ).astype(F32).astype(BF16)
        load_obs(b).wait()
        high, low = halves(obs[span, :].T)
        pieces[:chan, span] = high
        pieces[chan:2 * chan, span] = low
    pl.semaphore_wait(barrier, n - 1)

    each_wind(lambda s, w, l: load_wind(s, w, l).wait())
    for s in range(STEPS):
        col = jnp.zeros((lev, LANES), F32)
        for l in range(lat_rows):
            tile = winds[s, 0, l, :, lon_cols - LANES:]
            col = jnp.where(lane == l, tile[:, LANES - 1:], col)
        wind_send[s] = col

    @pl.when(lat == 0)
    def _():
        wind_row[...] = jnp.zeros_like(wind_row)
        for t in range(STEPS):
            row_halo[t, 0] = jnp.zeros((chan, lon_cols), F32)

    @pl.when(lat == n_lat - 1)
    def _():
        for t in range(STEPS):
            row_halo[t, 1] = jnp.zeros((chan, lon_cols), F32)

    east = (lat, lax.rem(lon + 1, n_lon))
    west = (lat, lax.rem(lon + n_lon - 1, n_lon))
    north = (lax.rem(lat + 1, n_lat), lon)
    south = (lax.rem(lat + n_lat - 1, n_lat), lon)

    send_wind_col = remote(wind_send, wind_col, ws_sem.at[0], wr_sem.at[0], east)
    send_wind_col.start()

    def wind_row_copy(s):
        return remote(
            winds.at[s, 1, lat_rows - 1], wind_row.at[s],
            ws_sem.at[1 + s], wr_sem.at[1 + s], north,
        )

    @pl.when(lat < n_lat - 1)
    def _():
        for s in range(STEPS):
            wind_row_copy(s).start()

    def message(ref, d, f):
        if f == 0:
            return ref.at[d, pl.ds(0, META + lev)]
        return ref.at[d, pl.ds(META + f * lev, lev)]

    def value_copy(d, f):
        return remote(
            message(send_v, d, f), message(recv_v, me, f),
            sv_sem.at[f, d], rv_sem.at[f, me], device(d),
        )

    def arrival(src, f):
        return remote(
            message(send_v, src, f), message(recv_v, src, f),
            sv_sem.at[f, src], rv_sem.at[f, src], device(src),
        )

    def own_copy():
        return pltpu.make_async_copy(send_v.at[me], recv_v.at[me], self_sem)

    def target(g):
        return lax.rem(me + TWIST * (g + 1), n)

    def source(g):
        return lax.rem(me + (n - TWIST % n) * (g + 1), n)

    def pack(p, _):
        hots = []
        for q in range(2):
            d = target(2 * p + q)
            slots = lax.broadcasted_iota(jnp.int32, (LANES, rows), 0) + d * LANES
            hots.append(jnp.where(slots == rank_ref[...], 1.0, 0.0).astype(BF16))
        both = lax.dot_general(
            pieces[...], jnp.concatenate(hots, axis=0), NT, preferred_element_type=F32
        )
        for q in range(2):
            d = target(2 * p + q)
            at = slice(q * LANES, (q + 1) * LANES)
            send_v[d, META:] = both[:chan, at] + both[chan:2 * chan, at]
            send_v[d, :META] = both[2 * chan:2 * chan + META, at]

            @pl.when(d != me)
            def _():
                value_copy(d, 0).start()

            @pl.when(d == me)
            def _():
                own_copy().start()

        return 0

    lax.fori_loop(0, n // 2, pack, 0)

    def send_field(f):
        def start(g, _):
            value_copy(target(g), f).start()
            return 0

        lax.fori_loop(0, n - 1, start, 0)

    if fields > 1:
        send_field(1)

    k_tile = jnp.broadcast_to(diffusion_ref[...], (LANES, chan)).T
    for j in range(lon_cols // LANES):
        k_ref[:, j * LANES:(j + 1) * LANES] = k_tile
    each_row(lambda l: load_row(l).wait())

    def skew(l, _):
        state_a[l] = pltpu.roll(state_a[l], l + 1, 1)
        return 0

    lax.fori_loop(0, lat_rows, skew, 0)

    def prepare():
        send_wind_col.wait()

        @pl.when(lat < n_lat - 1)
        def _():
            for s in range(STEPS):
                wind_row_copy(s).wait_send()

        @pl.when(lat > 0)
        def _():
            for s in range(STEPS):
                wind_row_copy(s).wait_recv()

        first = lax.broadcasted_iota(jnp.int32, (lev, lon_cols), 1) == 0
        for s in range(STEPS):
            def halve(l, _):
                u = winds[s, 0, l]
                edge = pltpu.roll(wind_col[s], lax.rem(LANES - l, LANES), 1)
                edge = jnp.concatenate([edge] * (lon_cols // LANES), axis=1)
                half[s, 0, l] = 0.5 * pltpu.roll(u, l + 1, 1)
                half[s, 1, l] = 0.5 * pltpu.roll(winds[s, 1, l], l + 1, 1)
                wind_west[s, l] = 0.5 * pltpu.roll(jnp.where(first, edge, pltpu.roll(u, 1, 1)), l + 1, 1)
                south_wind = winds[s, 1, jnp.maximum(l - 1, 0)]
                south_wind = jnp.where(l == 0, wind_row[s], south_wind)
                wind_south[s, l] = 0.5 * pltpu.roll(south_wind, l + 1, 1)
                return 0

            lax.fori_loop(0, lat_rows, halve, 0)

    def unpack_field(f):
        part = slice(f * lev, (f + 1) * lev)

        def unpack(p, _):
            for j in range(2 * JOIN):
                src = source(p * 2 * JOIN + j)

                @pl.when(src != me)
                def _():
                    arrival(src, f).wait_recv()

                if f == 0:
                    @pl.when(src == me)
                    def _():
                        own_copy().wait()

            for c in range(2):
                highs, lows, places = [], [], []
                for j in range(JOIN):
                    src = source((p * 2 + c) * JOIN + j)
                    high, low = halves(recv_v[src, META + f * lev:META + (f + 1) * lev])
                    highs.append(high)
                    lows.append(low)
                    places.append(recv_v[src, :META])
                values = jnp.concatenate(highs + lows, axis=1)
                cell = jnp.concatenate(places, axis=1)
                lons = lax.broadcasted_iota(jnp.int32, (lon_cols, cell.shape[1]), 0)
                hot = jnp.where(lons == cell[1:2].astype(jnp.int32), 1.0, 0.0).astype(BF16)
                hot = jnp.concatenate([hot, hot], axis=1)
                row = cell[0:1].astype(jnp.int32)
                row = jnp.concatenate([row, row], axis=1)
                for l in range(lat_rows):
                    mask = jnp.where(row == l, 1.0, 0.0).astype(BF16)
                    lhs[c, l * lev:(l + 1) * lev, :] = values * mask
                add = lax.dot_general(lhs[c], hot, NT, preferred_element_type=F32)
                for l in range(lat_rows):
                    state_a[l, part] += add[l * lev:(l + 1) * lev]
            return 0

        lax.fori_loop(0, n // (2 * JOIN), unpack, 0)

    def halo_copies(t, f):
        now = state_b if t % 2 else state_a
        part = pl.ds(f * lev, lev)
        pairs = (
            (now.at[lat_rows - 1, part], row_halo.at[t, 0, part], north),
            (now.at[0, part], row_halo.at[t, 1, part], south),
            (col_send.at[t, 0, part], col_halo.at[t, 0, part], east),
            (col_send.at[t, 1, part], col_halo.at[t, 1, part], west),
        )
        return [
            remote(src, dst, hs_sem.at[t, f, i], hr_sem.at[t, f, i], to)
            for i, (src, dst, to) in enumerate(pairs)
        ]

    def send_halos(t, f, low, high):
        part = slice(f * lev, (f + 1) * lev)
        to_north, to_south, to_east, to_west = halo_copies(t, f)

        @pl.when(lat < n_lat - 1)
        def _():
            to_north.start()

        @pl.when(lat > 0)
        def _():
            to_south.start()

        col_send[t, 0, part, :] = pltpu.roll(high, 1, 1)
        col_send[t, 1, part, :] = pltpu.roll(low, LANES - 1, 1)
        to_east.start()
        to_west.start()

    def wait_halos(t, f):
        to_north, to_south, to_east, to_west = halo_copies(t, f)

        @pl.when(lat > 0)
        def _():
            to_north.wait_recv()
            to_south.wait_send()

        @pl.when(lat < n_lat - 1)
        def _():
            to_south.wait_recv()
            to_north.wait_send()

        to_east.wait()
        to_west.wait()

    blank = jnp.zeros((lev, LANES), F32)

    def first_halos(f):
        part = slice(f * lev, (f + 1) * lev)
        low = high = blank
        for l in range(lat_rows):
            tile = state_a[l, part, :LANES]
            low = jnp.where(lane == l + 1, tile, low)
            high = jnp.where(lane == l, tile, high)
        send_halos(0, f, low, high)

    def head_of(x, at, ends):
        return jnp.concatenate([jnp.where(lane == at, ends, x[:, :LANES]), x[:, LANES:]], axis=1)

    def store_row(l, f):
        part = pl.ds(f * lev, lev)
        return pltpu.make_async_copy(
            state_b.at[l, part], out_ref.at[part, l, :], out_sem.at[f, l]
        )

    def advance(t, f):
        s = STEPS - 1 - t
        now, later = (state_a, state_b) if t % 2 == 0 else (state_b, state_a)
        part = slice(f * lev, (f + 1) * lev)
        wait_halos(t, f)
        k = k_ref[part, :]
        ends_west = col_halo[t, 0, part, :]
        ends_east = col_halo[t, 1, part, :]

        def row(l, below, core, e, above, low, high):
            w = pltpu.roll(core, 1, 1)
            new = core + (head_of(e, l, ends_east) - core) * (half[s, 0, l] + k)
            new = new + (core - head_of(w, l + 1, ends_west)) * (wind_west[s, l] - k)
            new = new + (above - core) * (half[s, 1, l] + k)
            new = new + (core - below) * (wind_south[s, l] - k)
            if t == STEPS - 1:
                later[l, part, :] = pltpu.roll(new, lon_cols - 1 - l, 1)
            else:
                later[l, part, :] = new
                low = jnp.where(lane == l + 1, new[:, :LANES], low)
                high = jnp.where(lane == l, new[:, :LANES], high)
            return w, low, high

        def inner(l, state):
            below, core, e, low, high = state
            following = now[l + 1, part, :]
            above = pltpu.roll(following, lon_cols - 1, 1)
            w, low, high = row(l, below, core, e, above, low, high)
            return w, following, above, low, high

        below = pltpu.roll(row_halo[t, 0, part, :], lon_cols - (lat_rows - 1), 1)
        core = now[0, part, :]
        e = pltpu.roll(core, lon_cols - 1, 1)
        below, core, e, low, high = lax.fori_loop(
            0, lat_rows - 1, inner, (below, core, e, blank, blank), unroll=UNROLL
        )
        above = pltpu.roll(row_halo[t, 1, part, :], lat_rows - 1, 1)
        _, low, high = row(lat_rows - 1, below, core, e, above, low, high)
        if t < STEPS - 1:
            send_halos(t + 1, f, low, high)
        else:
            each_row(lambda l: store_row(l, f).start())

    prepare()
    for slot in range(fields + STEPS):
        if slot < fields:
            unpack_field(slot)
            first_halos(slot)
            if slot + 2 < fields:
                send_field(slot + 2)
        for t in range(STEPS):
            f = slot - 1 - t
            if 0 <= f < fields:
                advance(t, f)

    for f in range(fields):
        def drain(g, _):
            value_copy(target(g), f).wait_send()
            return 0

        lax.fori_loop(0, n - 1, drain, 0)
        each_row(lambda l: store_row(l, f).wait())


def local(adjoint_in, obs_adjoint, obs_owner, obs_column, winds, diffusion):
    chan, lat_rows, lon_cols = adjoint_in.shape
    steps, _, lev = winds.shape[:3]
    n_lat = lax.axis_size("lat")
    n_lon = lax.axis_size("lon")
    n = n_lat * n_lon
    rows = obs_adjoint.shape[0]
    fields = chan // lev
    owner = obs_owner.reshape(1, rows)
    column = obs_column.reshape(1, rows)
    k = diffusion.reshape(1, chan)
    vmem = pl.BlockSpec(memory_space=pltpu.VMEM)
    hbm = pl.BlockSpec(memory_space=pl.ANY)
    dma = pltpu.SemaphoreType.DMA
    return pl.pallas_call(
        functools.partial(kernel, n_lat, n_lon),
        out_shape=jax.ShapeDtypeStruct((chan, lat_rows, lon_cols), F32),
        in_specs=[hbm, vmem, vmem, vmem, hbm, hbm],
        out_specs=hbm,
        scratch_shapes=[
            pltpu.VMEM((rows, chan), F32),
            pltpu.VMEM((chan, lon_cols), F32),
            pltpu.VMEM((steps, 2, lat_rows, lev, lon_cols), F32),
            pltpu.VMEM((steps, lat_rows, lev, lon_cols), F32),
            pltpu.VMEM((steps, lat_rows, lev, lon_cols), F32),
            pltpu.VMEM((2 * chan + 16, rows), BF16),
            pltpu.VMEM((1, rows), jnp.int32),
            pltpu.VMEM((n, META + chan, LANES), F32),
            pltpu.VMEM((n, META + chan, LANES), F32),
            pltpu.VMEM((2, lat_rows * lev, 2 * JOIN * LANES), BF16),
            pltpu.VMEM((lat_rows, chan, lon_cols), F32),
            pltpu.VMEM((lat_rows, chan, lon_cols), F32),
            pltpu.VMEM((steps, 2, lat_rows, lev, lon_cols), F32),
            pltpu.VMEM((steps, 2, chan, lon_cols), F32),
            pltpu.VMEM((steps, 2, chan, LANES), F32),
            pltpu.VMEM((steps, 2, chan, LANES), F32),
            pltpu.VMEM((steps, lev, lon_cols), F32),
            pltpu.VMEM((steps, lev, LANES), F32),
            pltpu.VMEM((steps, lev, LANES), F32),
            dma((rows // 256,)), dma((lat_rows,)), dma((steps, 2, lat_rows)), dma,
            dma((fields, n)), dma((fields, n)),
            dma((steps, fields, 4)), dma((steps, fields, 4)), dma((1 + steps,)), dma((1 + steps,)),
            dma((fields, lat_rows)),
        ],
        compiler_params=pltpu.CompilerParams(
            collective_id=0, has_side_effects=True, vmem_limit_bytes=60 * 1024 * 1024
        ),
    )(obs_adjoint, owner, column, k, adjoint_in, winds)


def solution(mesh):
    placed = (
        P(None, "lat", "lon"),
        P(("lat", "lon"), None),
        P(("lat", "lon"), None),
        P(("lat", "lon")),
        P(None, None, None, "lat", "lon"),
        P(),
    )
    return jax.shard_map(
        local, mesh=mesh, in_specs=placed, out_specs=P(None, "lat", "lon"), check_vma=False
    )
```

profile of v0, /device:TPU:20, one launch (start us, length us, event | category | flops | bytes accessed | tf_op | source)
XLA Modules:
  0.0 86.8 jit_solution(5119403804131513970)
XLA Ops:
  0.0 83.7 %shard_map.64 = f32[128,16,256]{2,1,0:T(8,128)} custom-call(f32[2048,128]{1,0:T(8,128)} %obs_ref.1, s32[1,2048]{1,0:T(1,128)} %bitcast.3, s32[1,2048]{1,0:T(1,128)} %bitcast.4, f32[1,128]{1,0:T(1,128)} %bitcast.5, f32[128,16,256]{2,1,0:T(8,128)} %adj_ref.1, f32[3,2,32,16,256]{4,3,2,1,0:T(8,128)} %winds_ref.1), custom_call_target="tpu_custom_call" | custom-call | tf_op jit(solution)/shard_map/pallas_call | solution.py:448
  83.7 3.1 %copy.8 = f32[128,16,256]{2,1,0:T(8,128)} copy(f32[128,16,256]{2,1,0:T(8,128)} %shard_map.64) | data formatting | bytes 4194304
where the time goes:
time: 87.8 us; the launch traced here: 86.8 us
  Pallas kernels  83.7 us (95%)
  local copies, waits for them, and re-layouts  3.08 us (4%)
    pallas_call x1, Pallas kernels, local(): pl.pallas_call(functools.partial(kernel, n_lat, n_lon), out_shape=jax.Sha...  83.7 us
    unnamed x1, local copies, waits for them, and re-layouts  3.08 us

commit v1 on v0

--- a/solution.py
+++ b/solution.py
@@ -9,15 +9,25 @@
 
 STEPS = 3
 LANES = 128
-META = 8
+SPLIT = 0
 JOIN = 4
 TWIST = 13
-UNROLL = 5
+UNROLL = 7
 F32 = jnp.float32
 BF16 = jnp.bfloat16
 NT = (((1,), (1,)), ((), ()))
 
 
+def plan(chan, lev):
+    fields = chan // lev
+    cut = lev // 2 if lev % 16 == 0 else lev
+    sizes = [lev if f < fields - SPLIT else cut for f in range(fields)]
+    return [
+        (f * lev + at, at, size)
+        for f, size in enumerate(sizes) for at in range(0, lev, size)
+    ]
+
+
 def halves(x):
     high = x.astype(BF16)
     return high, (x - high.astype(F32)).astype(BF16)
@@ -26,9 +36,9 @@
 def kernel(
     n_lat, n_lon,
     obs_ref, owner_ref, column_ref, diffusion_ref, adj_ref, winds_ref, out_ref,
-    obs, k_ref, half, wind_west, wind_south, pieces, rank_ref, send_v, recv_v, lhs,
+    obs, k_ref, half, wind_west, wind_south, pieces, rank_ref, send_v, recv_v, send_c, recv_c, lhs,
     state_a, state_b, winds, row_halo, col_send, col_halo, wind_row, wind_send, wind_col,
-    obs_sem, adj_sem, wind_sem, self_sem, sv_sem, rv_sem, hs_sem, hr_sem, ws_sem, wr_sem, out_sem,
+    obs_sem, adj_sem, wind_sem, self_sem, sv_sem, rv_sem, sc_sem, rc_sem, hs_sem, hr_sem, ws_sem, wr_sem, out_sem,
 ):
     lat = lax.axis_index("lat")
     lon = lax.axis_index("lon")
@@ -37,7 +47,7 @@
     rows, chan = obs.shape
     lat_rows, _, lon_cols = state_a.shape
     lev = winds.shape[3]
-    fields = chan // lev
+    chunks = plan(chan, lev)
     lane = lax.broadcasted_iota(jnp.int32, (1, LANES), 1)
 
     def device(d):
@@ -118,48 +128,9 @@
         pieces[chan:2 * chan, span] = low
     pl.semaphore_wait(barrier, n - 1)
 
-    each_wind(lambda s, w, l: load_wind(s, w, l).wait())
-    for s in range(STEPS):
-        col = jnp.zeros((lev, LANES), F32)
-        for l in range(lat_rows):
-            tile = winds[s, 0, l, :, lon_cols - LANES:]
-            col = jnp.where(lane == l, tile[:, LANES - 1:], col)
-        wind_send[s] = col
-
-    @pl.when(lat == 0)
-    def _():
-        wind_row[...] = jnp.zeros_like(wind_row)
-        for t in range(STEPS):
-            row_halo[t, 0] = jnp.zeros((chan, lon_cols), F32)
-
-    @pl.when(lat == n_lat - 1)
-    def _():
-        for t in range(STEPS):
-            row_halo[t, 1] = jnp.zeros((chan, lon_cols), F32)
-
-    east = (lat, lax.rem(lon + 1, n_lon))
-    west = (lat, lax.rem(lon + n_lon - 1, n_lon))
-    north = (lax.rem(lat + 1, n_lat), lon)
-    south = (lax.rem(lat + n_lat - 1, n_lat), lon)
-
-    send_wind_col = remote(wind_send, wind_col, ws_sem.at[0], wr_sem.at[0], east)
-    send_wind_col.start()
-
-    def wind_row_copy(s):
-        return remote(
-            winds.at[s, 1, lat_rows - 1], wind_row.at[s],
-            ws_sem.at[1 + s], wr_sem.at[1 + s], north,
-        )
-
-    @pl.when(lat < n_lat - 1)
-    def _():
-        for s in range(STEPS):
-            wind_row_copy(s).start()
-
     def message(ref, d, f):
-        if f == 0:
-            return ref.at[d, pl.ds(0, META + lev)]
-        return ref.at[d, pl.ds(META + f * lev, lev)]
+        base, _, size = chunks[f]
+        return ref.at[d, pl.ds(base, size)]
 
     def value_copy(d, f):
         return remote(
@@ -173,8 +144,17 @@
             sv_sem.at[f, src], rv_sem.at[f, src], device(src),
         )
 
-    def own_copy():
-        return pltpu.make_async_copy(send_v.at[me], recv_v.at[me], self_sem)
+    def cell_copy(d):
+        return remote(send_c.at[d], recv_c.at[me], sc_sem.at[d], rc_sem.at[me], device(d))
+
+    def cell_arrival(src):
+        return remote(send_c.at[src], recv_c.at[src], sc_sem.at[src], rc_sem.at[src], device(src))
+
+    def own_copies():
+        return (
+            pltpu.make_async_copy(send_v.at[me], recv_v.at[me], self_sem.at[0]),
+            pltpu.make_async_copy(send_c.at[me], recv_c.at[me], self_sem.at[1]),
+        )
 
     def target(g):
         return lax.rem(me + TWIST * (g + 1), n)
@@ -194,20 +174,60 @@
         for q in range(2):
             d = target(2 * p + q)
             at = slice(q * LANES, (q + 1) * LANES)
-            send_v[d, META:] = both[:chan, at] + both[chan:2 * chan, at]
-            send_v[d, :META] = both[2 * chan:2 * chan + META, at]
+            send_v[d] = both[:chan, at] + both[chan:2 * chan, at]
+            send_c[d] = both[2 * chan:2 * chan + 1, at] * lon_cols + both[2 * chan + 1:2 * chan + 2, at]
 
             @pl.when(d != me)
             def _():
+                cell_copy(d).start()
                 value_copy(d, 0).start()
 
             @pl.when(d == me)
             def _():
-                own_copy().start()
+                for copy in own_copies():
+                    copy.start()
 
         return 0
 
-    lax.fori_loop(0, n // 2, pack, 0)
+    lax.fori_loop(0, 1, pack, 0)
+    each_wind(lambda s, w, l: load_wind(s, w, l).wait())
+    for s in range(STEPS):
+        col = jnp.zeros((lev, LANES), F32)
+        for l in range(lat_rows):
+            tile = winds[s, 0, l, :, lon_cols - LANES:]
+            col = jnp.where(lane == l, tile[:, LANES - 1:], col)
+        wind_send[s] = col
+
+    @pl.when(lat == 0)
+    def _():
+        wind_row[...] = jnp.zeros_like(wind_row)
+        for t in range(STEPS):
+            row_halo[t, 0] = jnp.zeros((chan, lon_cols), F32)
+
+    @pl.when(lat == n_lat - 1)
+    def _():
+        for t in range(STEPS):
+            row_halo[t, 1] = jnp.zeros((chan, lon_cols), F32)
+
+    east = (lat, lax.rem(lon + 1, n_lon))
+    west = (lat, lax.rem(lon + n_lon - 1, n_lon))
+    north = (lax.rem(lat + 1, n_lat), lon)
+    south = (lax.rem(lat + n_lat - 1, n_lat), lon)
+
+    send_wind_col = remote(wind_send, wind_col, ws_sem.at[0], wr_sem.at[0], east)
+    send_wind_col.start()
+
+    def wind_row_copy(s):
+        return remote(
+            winds.at[s, 1, lat_rows - 1], wind_row.at[s],
+            ws_sem.at[1 + s], wr_sem.at[1 + s], north,
+        )
+
+    @pl.when(lat < n_lat - 1)
+    def _():
+        for s in range(STEPS):
+            wind_row_copy(s).start()
+    lax.fori_loop(1, n // 2, pack, 0)
 
     def send_field(f):
         def start(g, _):
@@ -216,7 +236,7 @@
 
         lax.fori_loop(0, n - 1, start, 0)
 
-    if fields > 1:
+    if len(chunks) > 1:
         send_field(1)
 
     k_tile = jnp.broadcast_to(diffusion_ref[...], (LANES, chan)).T
@@ -260,7 +280,8 @@
             lax.fori_loop(0, lat_rows, halve, 0)
 
     def unpack_field(f):
-        part = slice(f * lev, (f + 1) * lev)
+        base, _, size = chunks[f]
+        part = slice(base, base + size)
 
         def unpack(p, _):
             for j in range(2 * JOIN):
@@ -269,40 +290,46 @@
                 @pl.when(src != me)
                 def _():
                     arrival(src, f).wait_recv()
+                    if f == 0:
+                        cell_arrival(src).wait_recv()
 
                 if f == 0:
                     @pl.when(src == me)
                     def _():
-                        own_copy().wait()
+                        for copy in own_copies():
+                            copy.wait()
 
             for c in range(2):
                 highs, lows, places = [], [], []
                 for j in range(JOIN):
                     src = source((p * 2 + c) * JOIN + j)
-                    high, low = halves(recv_v[src, META + f * lev:META + (f + 1) * lev])
+                    high, low = halves(recv_v[src, base:base + size])
                     highs.append(high)
                     lows.append(low)
-                    places.append(recv_v[src, :META])
+                    places.append(recv_c[src])
                 values = jnp.concatenate(highs + lows, axis=1)
                 cell = jnp.concatenate(places, axis=1)
                 lons = lax.broadcasted_iota(jnp.int32, (lon_cols, cell.shape[1]), 0)
-                hot = jnp.where(lons == cell[1:2].astype(jnp.int32), 1.0, 0.0).astype(BF16)
+                row = jnp.floor((cell + 0.5) * (1.0 / lon_cols))
+                turned = (cell - row * lon_cols).astype(jnp.int32)
+                hot = jnp.where(lons == turned, 1.0, 0.0).astype(BF16)
                 hot = jnp.concatenate([hot, hot], axis=1)
-                row = cell[0:1].astype(jnp.int32)
+                row = row.astype(jnp.int32)
                 row = jnp.concatenate([row, row], axis=1)
                 for l in range(lat_rows):
                     mask = jnp.where(row == l, 1.0, 0.0).astype(BF16)
-                    lhs[c, l * lev:(l + 1) * lev, :] = values * mask
-                add = lax.dot_general(lhs[c], hot, NT, preferred_element_type=F32)
+                    lhs[c, l * size:(l + 1) * size, :] = values * mask
+                add = lax.dot_general(lhs[c, :lat_rows * size], hot, NT, preferred_element_type=F32)
                 for l in range(lat_rows):
-                    state_a[l, part] += add[l * lev:(l + 1) * lev]
+                    state_a[l, part] += add[l * size:(l + 1) * size]
             return 0
 
         lax.fori_loop(0, n // (2 * JOIN), unpack, 0)
 
     def halo_copies(t, f):
         now = state_b if t % 2 else state_a
-        part = pl.ds(f * lev, lev)
+        base, _, size = chunks[f]
+        part = pl.ds(base, size)
         pairs = (
             (now.at[lat_rows - 1, part], row_halo.at[t, 0, part], north),
             (now.at[0, part], row_halo.at[t, 1, part], south),
@@ -314,9 +341,8 @@
             for i, (src, dst, to) in enumerate(pairs)
         ]
 
-    def send_halos(t, f, low, high):
-        part = slice(f * lev, (f + 1) * lev)
-        to_north, to_south, to_east, to_west = halo_copies(t, f)
+    def send_rows(t, f):
+        to_north, to_south, _, _ = halo_copies(t, f)
 
         @pl.when(lat < n_lat - 1)
         def _():
@@ -326,6 +352,10 @@
         def _():
             to_south.start()
 
+    def send_columns(t, f, low, high):
+        base, _, size = chunks[f]
+        part = slice(base, base + size)
+        _, _, to_east, to_west = halo_copies(t, f)
         col_send[t, 0, part, :] = pltpu.roll(high, 1, 1)
         col_send[t, 1, part, :] = pltpu.roll(low, LANES - 1, 1)
         to_east.start()
@@ -333,6 +363,8 @@
 
     def wait_halos(t, f):
         to_north, to_south, to_east, to_west = halo_copies(t, f)
+        to_east.wait()
+        to_west.wait()
 
         @pl.when(lat > 0)
         def _():
@@ -344,25 +376,23 @@
             to_south.wait_recv()
             to_north.wait_send()
 
-        to_east.wait()
-        to_west.wait()
-
-    blank = jnp.zeros((lev, LANES), F32)
-
     def first_halos(f):
-        part = slice(f * lev, (f + 1) * lev)
-        low = high = blank
+        base, _, size = chunks[f]
+        part = slice(base, base + size)
+        send_rows(0, f)
+        low = high = jnp.zeros((size, LANES), F32)
         for l in range(lat_rows):
             tile = state_a[l, part, :LANES]
             low = jnp.where(lane == l + 1, tile, low)
             high = jnp.where(lane == l, tile, high)
-        send_halos(0, f, low, high)
+        send_columns(0, f, low, high)
 
     def head_of(x, at, ends):
         return jnp.concatenate([jnp.where(lane == at, ends, x[:, :LANES]), x[:, LANES:]], axis=1)
 
     def store_row(l, f):
-        part = pl.ds(f * lev, lev)
+        base, _, size = chunks[f]
+        part = pl.ds(base, size)
         return pltpu.make_async_copy(
             state_b.at[l, part], out_ref.at[part, l, :], out_sem.at[f, l]
         )
@@ -370,19 +400,26 @@
     def advance(t, f):
         s = STEPS - 1 - t
         now, later = (state_a, state_b) if t % 2 == 0 else (state_b, state_a)
-        part = slice(f * lev, (f + 1) * lev)
+        base, level, size = chunks[f]
+        part = slice(base, base + size)
+        levs = slice(level, level + size)
+        final = t == STEPS - 1
+        last = lat_rows - 1
         wait_halos(t, f)
         k = k_ref[part, :]
         ends_west = col_halo[t, 0, part, :]
         ends_east = col_halo[t, 1, part, :]
 
+        def left(x):
+            return pltpu.roll(x, lon_cols - 1, 1)
+
         def row(l, below, core, e, above, low, high):
             w = pltpu.roll(core, 1, 1)
-            new = core + (head_of(e, l, ends_east) - core) * (half[s, 0, l] + k)
-            new = new + (core - head_of(w, l + 1, ends_west)) * (wind_west[s, l] - k)
-            new = new + (above - core) * (half[s, 1, l] + k)
-            new = new + (core - below) * (wind_south[s, l] - k)
-            if t == STEPS - 1:
+            new = core + (head_of(e, l, ends_east) - core) * (half[s, 0, l, levs] + k)
+            new = new + (core - head_of(w, l + 1, ends_west)) * (wind_west[s, l, levs] - k)
+            new = new + (above - core) * (half[s, 1, l, levs] + k)
+            new = new + (core - below) * (wind_south[s, l, levs] - k)
+            if final:
                 later[l, part, :] = pltpu.roll(new, lon_cols - 1 - l, 1)
             else:
                 later[l, part, :] = new
@@ -393,38 +430,47 @@
         def inner(l, state):
             below, core, e, low, high = state
             following = now[l + 1, part, :]
-            above = pltpu.roll(following, lon_cols - 1, 1)
+            above = left(following)
             w, low, high = row(l, below, core, e, above, low, high)
             return w, following, above, low, high
 
-        below = pltpu.roll(row_halo[t, 0, part, :], lon_cols - (lat_rows - 1), 1)
+        low = high = jnp.zeros((size, LANES), F32)
+        below = pltpu.roll(row_halo[t, 0, part, :], lon_cols - last, 1)
         core = now[0, part, :]
-        e = pltpu.roll(core, lon_cols - 1, 1)
-        below, core, e, low, high = lax.fori_loop(
-            0, lat_rows - 1, inner, (below, core, e, blank, blank), unroll=UNROLL
-        )
-        above = pltpu.roll(row_halo[t, 1, part, :], lat_rows - 1, 1)
-        _, low, high = row(lat_rows - 1, below, core, e, above, low, high)
-        if t < STEPS - 1:
-            send_halos(t + 1, f, low, high)
+        following = now[1, part, :]
+        e = left(following)
+        w, low, high = row(0, below, core, left(core), e, low, high)
+        below = pltpu.roll(now[last - 1, part, :], 1, 1)
+        core = now[last, part, :]
+        above = pltpu.roll(row_halo[t, 1, part, :], last, 1)
+        _, low, high = row(last, below, core, left(core), above, low, high)
+        if not final:
+            send_rows(t + 1, f)
+        _, _, _, low, high = lax.fori_loop(
+            1, last, inner, (w, following, e, low, high), unroll=UNROLL
+        )
+        if final:
+            each_row(lambda l: store_row(l, f).start())
         else:
-            each_row(lambda l: store_row(l, f).start())
+            send_columns(t + 1, f, low, high)
 
     prepare()
-    for slot in range(fields + STEPS):
-        if slot < fields:
+    for slot in range(len(chunks) + STEPS):
+        if slot < len(chunks):
+            if slot + 2 < len(chunks):
+                send_field(slot + 2)
             unpack_field(slot)
             first_halos(slot)
-            if slot + 2 < fields:
-                send_field(slot + 2)
         for t in range(STEPS):
             f = slot - 1 - t
-            if 0 <= f < fields:
+            if 0 <= f < len(chunks):
                 advance(t, f)
 
-    for f in range(fields):
+    for f in range(len(chunks)):
         def drain(g, _):
             value_copy(target(g), f).wait_send()
+            if f == 0:
+                cell_copy(target(g)).wait_send()
             return 0
 
         lax.fori_loop(0, n - 1, drain, 0)
@@ -438,18 +484,18 @@
     n_lon = lax.axis_size("lon")
     n = n_lat * n_lon
     rows = obs_adjoint.shape[0]
-    fields = chan // lev
+    parts = len(plan(chan, lev))
     owner = obs_owner.reshape(1, rows)
     column = obs_column.reshape(1, rows)
     k = diffusion.reshape(1, chan)
     vmem = pl.BlockSpec(memory_space=pltpu.VMEM)
-    hbm = pl.BlockSpec(memory_space=pl.ANY)
+    hbm = pl.BlockSpec(memory_space=pltpu.HBM)
     dma = pltpu.SemaphoreType.DMA
     return pl.pallas_call(
         functools.partial(kernel, n_lat, n_lon),
-        out_shape=jax.ShapeDtypeStruct((chan, lat_rows, lon_cols), F32),
+        out_shape=pltpu.VMEM((chan, lat_rows, lon_cols), F32),
         in_specs=[hbm, vmem, vmem, vmem, hbm, hbm],
-        out_specs=hbm,
+        out_specs=vmem,
         scratch_shapes=[
             pltpu.VMEM((rows, chan), F32),
             pltpu.VMEM((chan, lon_cols), F32),
@@ -458,8 +504,10 @@
             pltpu.VMEM((steps, lat_rows, lev, lon_cols), F32),
             pltpu.VMEM((2 * chan + 16, rows), BF16),
             pltpu.VMEM((1, rows), jnp.int32),
-            pltpu.VMEM((n, META + chan, LANES), F32),
-            pltpu.VMEM((n, META + chan, LANES), F32),
+            pltpu.VMEM((n, chan, LANES), F32),
+            pltpu.VMEM((n, chan, LANES), F32),
+            pltpu.VMEM((n, 1, LANES), F32),
+            pltpu.VMEM((n, 1, LANES), F32),
             pltpu.VMEM((2, lat_rows * lev, 2 * JOIN * LANES), BF16),
             pltpu.VMEM((lat_rows, chan, lon_cols), F32),
             pltpu.VMEM((lat_rows, chan, lon_cols), F32),
@@ -470,10 +518,10 @@
             pltpu.VMEM((steps, lev, lon_cols), F32),
             pltpu.VMEM((steps, lev, LANES), F32),
             pltpu.VMEM((steps, lev, LANES), F32),
-            dma((rows // 256,)), dma((lat_rows,)), dma((steps, 2, lat_rows)), dma,
-            dma((fields, n)), dma((fields, n)),
-            dma((steps, fields, 4)), dma((steps, fields, 4)), dma((1 + steps,)), dma((1 + steps,)),
-            dma((fields, lat_rows)),
+            dma((rows // 256,)), dma((lat_rows,)), dma((steps, 2, lat_rows)), dma((2,)),
+            dma((parts, n)), dma((parts, n)), dma((n,)), dma((n,)),
+            dma((steps, parts, 4)), dma((steps, parts, 4)), dma((1 + steps,)), dma((1 + steps,)),
+            dma((parts, lat_rows)),
         ],
         compiler_params=pltpu.CompilerParams(
             collective_id=0, has_side_effects=True, vmem_limit_bytes=60 * 1024 * 1024

time: 87.8 us -> 84.1 us (0.958)
  Pallas kernels: 83.7 us -> 81.1 us
  local copies, waits for them, and re-layouts: 3.08 us -> 1.32 us
    pallas_call x1, Pallas kernels: 83.7 us -> 81.1 us  [local(): pl.pallas_call(functools.partial(kernel, n_lat, n_lon), out_shape=pltpu.V...]
    unnamed x1, local copies, waits for them, and re-layouts: 3.08 us -> 1.32 us
where the time goes in v1:
time: 84.1 us; the launch traced here: 82.5 us
  Pallas kernels  81.1 us (96%)
  local copies, waits for them, and re-layouts  1.32 us (2%)
    pallas_call x1, Pallas kernels, local(): pl.pallas_call(functools.partial(kernel, n_lat, n_lon), out_shape=pltpu.V...  81.1 us

profile of v1, /device:TPU:20, one launch (start us, length us, event | category | flops | bytes accessed | tf_op | source)
XLA Modules:
  0.0 82.5 jit_solution(906292693452905766)
XLA Ops:
  0.0 81.1 %shard_map.64 = f32[128,16,256]{2,1,0:T(8,128)S(1)} custom-call(f32[2048,128]{1,0:T(8,128)} %obs_ref.1, s32[1,2048]{1,0:T(1,128)} %bitcast.3, s32[1,2048]{1,0:T(1,128)} %bitcast.4, f32[1,128]{1,0:T(1,128)} %bitcast.5, f32[128,16,256]{2,1,0:T(8,128)} %adj_ref.1, f32[3,2,32,16,256]{4,3,2,1,0:T(8,128)} %winds_ref.1), custom_call_target="tpu_custom_call" | custom-call | tf_op jit(solution)/shard_map/pallas_call | solution.py:494
  81.2 1.3 %copy.8 = f32[128,16,256]{2,1,0:T(8,128)} copy(f32[128,16,256]{2,1,0:T(8,128)S(1)} %shard_map.64) | data formatting | bytes 4194304
